TPU v7x, 256 devices: a whole 4x4x8 slice. The times are simulated.
256 devices in a mesh: tm: 8 (over z), row: 4 (over y), col: 8 (over x, core).
Axes of the slice: x: 4, y: 4, z: 8, core: 2. Of those that a mesh axis runs over, the one named last changes fastest.
Arguments:
- latent: bfloat16 [32, 64, 192, 256], P('tm', 'row', 'col'), may hold values from -43 to 43
- gain_first: float32 [256], replicated, may hold values from 0.5 to 1.5
- bias_first: float32 [256], replicated, may hold values from -3 to 3
- kernel_first: bfloat16 [3, 3, 3, 256, 256], replicated, may hold values from -0.078125 to 0.078125
- gain_second: float32 [256], replicated, may hold values from 0.5 to 1.5
- bias_second: float32 [256], replicated, may hold values from -3 to 3
- kernel_second: bfloat16 [3, 3, 3, 256, 256], replicated, may hold values from -0.078125 to 0.078125
- conv_bias: float32 [256], replicated, may hold values from -3 to 3
Outputs:
- upsampled: bfloat16 [32, 128, 384, 256], P('tm', 'row', 'col')
All inputs are finite; a program needn't handle non-finite values.
Results may differ from a plain program's by a relative error of at most 0.006.
Values may be sent and summed in bfloat16 or wider, within the bound.
A program may use at most 64 MiB of HBM per device.

v0:
```python
import jax
import jax.numpy as jnp
from jax import lax
from jax.sharding import PartitionSpec as P

C = 256
GROUPS = 32
EPSILON = 1e-06


def entering(x, axis, combine, identity):
    peers, here = (lax.axis_size(axis), lax.axis_index(axis))
    everything = jax.tree.map(lambda part: lax.all_gather(part, axis), x)
    start = jax.tree.map(
        lambda part, zero: jnp.broadcast_to(jnp.asarray(zero, part.dtype), part.shape), x, identity
    )

    def hop(k, before):
        reached = k < here
        new = combine(before, jax.tree.map(lambda part: part[k], everything))
        return jax.tree.map(lambda a, b: jnp.where(reached, a, b), new, before)

    return lax.fori_loop(0, peers, hop, start)


def from_behind(block, axis, distance):
    devices = range(lax.axis_size(axis))
    route = [(i - distance, i) for i in devices if i - distance in devices]
    return lax.ppermute(block, axis, route)


def extended(x, sides, width):
    for axis, dim in sides:
        peers, length = (lax.axis_size(axis), x.shape[dim])
        up = [(i, (i + 1) % peers) for i in range(peers - 1)]
        down = [(j, i) for i, j in up]
        last = lax.slice_in_dim(x, length - width, length, axis=dim)
        leading = lax.slice_in_dim(x, 0, width, axis=dim)
        before = lax.ppermute(last, axis, up)
        after = lax.ppermute(leading, axis, down)
        x = jnp.concatenate([before, x, after], axis=dim)
    return x


def channel_terms(group_sum, group_square, cell_count):
    group_mean = group_sum / cell_count
    norm_scale = lax.rsqrt(group_square / cell_count - group_mean * group_mean + EPSILON)
    return (jnp.repeat(group_mean, C // GROUPS), jnp.repeat(norm_scale, C // GROUPS))


def add_pair(leading, trailing):
    return (leading[0] + trailing[0], leading[1] + trailing[1])


def span_moments(source):
    values = source.astype(jnp.float32)
    grouped = values.reshape(-1, GROUPS, C // GROUPS)
    local_sum = jnp.sum(grouped, axis=(0, 2))
    local_square = jnp.sum(grouped * grouped, axis=(0, 2))
    span_index = lax.axis_index("tm")
    tile_sum, tile_square = lax.psum((local_sum, local_square), ("row", "col"))
    empty_vec = jnp.zeros_like(tile_sum)
    prior_sum, prior_square = entering(
        (tile_sum, tile_square), "tm", add_pair, (empty_vec, empty_vec)
    )
    upto_sum = prior_sum + tile_sum
    upto_square = prior_square + tile_square
    per_span = (
        source.shape[0]
        * source.shape[1]
        * lax.axis_size("row")
        * source.shape[2]
        * lax.axis_size("col")
        * (C // GROUPS)
    )
    span_done = span_index.astype(jnp.float32)
    prior_terms = channel_terms(prior_sum, prior_square, jnp.maximum(span_done, 1.0) * per_span)
    upto_terms = channel_terms(upto_sum, upto_square, (span_done + 1.0) * per_span)
    return (prior_terms, upto_terms)


def widen_block(own_block):
    frame_cache = from_behind(own_block[-2:], "tm", 1)
    longer = jnp.concatenate([frame_cache, own_block], 0)
    return extended(longer, (("row", 1), ("col", 2)), 1)


def norm_conv_input(source, norm_gain, norm_bias):
    prior_terms, upto_terms = span_moments(source)
    values = source.astype(jnp.float32)
    activated = jax.nn.silu(
        (values - upto_terms[0]) * (upto_terms[1] * norm_gain) + norm_bias
    ).astype(jnp.bfloat16)
    return widen_block(activated)


def conv_block(padded, kernel):
    span_frames = padded.shape[0] - 2
    tile_rows = padded.shape[1] - 2
    tile_cols = padded.shape[2] - 2
    channels = padded.shape[3]
    running = jnp.zeros((span_frames * tile_rows * tile_cols, kernel.shape[-1]), jnp.float32)
    for tap_row in range(3):
        for tap_col in range(3):
            window = padded[:, tap_row : tap_row + tile_rows, tap_col : tap_col + tile_cols, :]
            stacked = jnp.concatenate(
                [window[tap_time : tap_time + span_frames] for tap_time in range(3)], axis=3
            )
            running = running + jnp.dot(
                stacked.reshape(-1, 3 * channels),
                kernel[:, tap_row, tap_col].reshape(3 * channels, -1),
                preferred_element_type=jnp.float32,
            )
    return running.reshape(span_frames, tile_rows, tile_cols, -1)


def on_device(
    latent, gain_first, bias_first, kernel_first, gain_second, bias_second, kernel_second, conv_bias
):
    hidden = conv_block(norm_conv_input(latent, gain_first, bias_first), kernel_first).astype(
        jnp.bfloat16
    )
    branch = conv_block(norm_conv_input(hidden, gain_second, bias_second), kernel_second)
    summed = (latent.astype(jnp.float32) + branch + conv_bias).astype(jnp.bfloat16)
    return jnp.repeat(jnp.repeat(summed, 2, axis=1), 2, axis=2)


def solution(mesh):
    return jax.shard_map(
        on_device,
        mesh=mesh,
        in_specs=(P("tm", "row", "col", None), P(), P(), P(), P(), P(), P(), P()),
        out_specs=P("tm", "row", "col", None),
        check_vma=False,
    )
```

profile of v0, /device:TPU:42, one launch (start us, length us, event | category | flops | bytes accessed | tf_op | source)
XLA Modules:
  0.0 261.2 jit_solution(14331374951814830136)
XLA Ops:
  0.0 1.4 fusion.6
  1.8 51.2 %all-reduce.5 = (f32[32]{0:T(128)S(1)}, f32[32]{0:T(128)S(1)}) all-reduce(f32[32]{0:T(128)S(1)} %reduce_sum.51, f32[32]{0:T(128)S(1)} %reduce_sum.54), channel_id=1, replica_groups=mesh['tm'=8,'row'=4,'col'=8] {'row','col'}, use_global_device_ids=true, to_apply=%region_2.0 | all-reduce | flops 64 | bytes 512 | tf_op jit(solution)/shard_map/psum | solution.py:61
  53.0 1.3 dynamic-slice
  55.4 17.9 %all-reduce.7 = (f32[256]{0:T(256)S(1)}, f32[256]{0:T(256)S(1)}) all-reduce(f32[256]{0:T(256)S(1)} %dynamic-update-slice, f32[256]{0:T(256)S(1)} %dynamic-update-slice.1), channel_id=2, replica_groups=mesh['tm'=8,'row'=4,'col'=8] {'tm'}, use_global_device_ids=true, to_apply=%add | all-reduce | flops 512 | bytes 4096
  74.8 1.6 fusion.14
  76.5 2.9 %collective-permute-start = (bf16[2,16,24,256]{3,2,1,0:T(8,128)(2,1)S(1)}, bf16[2,16,24,256]{3,2,1,0:T(8,128)(2,1)S(1)}, u32[]{:S(2)}, u32[]{:S(2)}) collective-permute-start(bf16[2,16,24,256]{3,2,1,0:T(8,128)(2,1)S(1)} %slice.400), channel_id=1, source_target_pairs={{0,32},{32,64},{64,96},{96,128},{128,160},{160,192},{192,224},{1,3... | collective-permute-start | bytes 1179656 | tf_op jit(solution)/shard_map/ppermute | solution.py:29
  79.4 2.3 fusion.20
  81.8 4.4 %collective-permute-done = bf16[2,16,24,256]{3,2,1,0:T(8,128)(2,1)S(1)} collective-permute-done((bf16[2,16,24,256]{3,2,1,0:T(8,128)(2,1)S(1)}, bf16[2,16,24,256]{3,2,1,0:T(8,128)(2,1)S(1)}, u32[]{:S(2)}, u32[]{:S(2)}) %collective-permute-start) | collective-permute-done | bytes 393248 | tf_op jit(solution)/shard_map/ppermute | solution.py:29
  86.2 13.4 %collective-permute-start.2 = (bf16[6,1,24,256]{3,2,1,0:T(8,128)(2,1)S(1)}, bf16[6,1,24,256]{3,2,1,0:T(8,128)(2,1)S(1)}, u32[]{:S(2)}, u32[]{:S(2)}) collective-permute-start(bf16[6,1,24,256]{3,2,1,0:T(8,128)(2,1)S(1)} %get-tuple-element.396), channel_id=1, source_target_pairs={{8,0},{16,8},{24,16},{9,1},{17,9},{25,17},{10,2},{18,10},{26,18},{... | collective-permute-start | bytes 221192 | tf_op jit(solution)/shard_map/ppermute | solution.py:40
  99.6 1.9 collective-permute-start.1
  101.7 4.1 %collective-permute-done.1 = bf16[6,1,24,256]{3,2,1,0:T(8,128)(2,1)S(1)} collective-permute-done((bf16[6,1,24,256]{3,2,1,0:T(8,128)(2,1)S(1)}, bf16[6,1,24,256]{3,2,1,0:T(8,128)(2,1)S(1)}, u32[]{:S(2)}, u32[]{:S(2)}) %collective-permute-start.1) | collective-permute-done | bytes 73760 | tf_op jit(solution)/shard_map/ppermute | solution.py:39
  106.0 1.9 collective-permute-start.4
  107.9 2.6 collective-permute-start.3
  111.4 6.5 %collective-permute-done.3 = bf16[6,18,1,256]{3,2,1,0:T(2,128)(2,1)S(1)} collective-permute-done((bf16[6,18,1,256]{3,2,1,0:T(2,128)(2,1)S(1)}, bf16[6,18,1,256]{3,2,1,0:T(2,128)(2,1)S(1)}, u32[]{:S(2)}, u32[]{:S(2)}) %collective-permute-start.3) | collective-permute-done | bytes 55328 | tf_op jit(solution)/shard_map/ppermute | solution.py:39
  117.9 1.2 pad_maximum_fusion.18
  119.7 5.1 %fusion.23 = (bf16[4,16,24,256]{3,2,1,0:T(8,128)(2,1)S(1)}, bf16[4,16,24,256]{3,2,1,0:T(8,128)(2,1)S(1)}, bf16[4,16,24,256]{3,2,1,0:T(8,128)(2,1)S(1)}, bf16[4,1...) fusion(bf16[6,18,25,256]{3,2,1,0:T(8,128)(2,1)S(1)} %get-tuple-, ...), kind=kLoop, calls=%fused_computation.101 | loop fusion | bytes 14155776 | tf_op jit(solution)/shard_map/slice | solution.py:107
  133.5 48.6 %all-reduce.4 = (f32[32]{0:T(128)S(1)}, f32[32]{0:T(128)S(1)}) all-reduce(f32[32]{0:T(128)S(1)} %reduce_sum.72, f32[32]{0:T(128)S(1)} %reduce_sum.75), channel_id=1, replica_groups=mesh['tm'=8,'row'=4,'col'=8] {'row','col'}, use_global_device_ids=true, to_apply=%region_10.11 | all-reduce | flops 64 | bytes 512 | tf_op jit(solution)/shard_map/psum | solution.py:61
  182.5 15.1 %all-reduce.6 = (f32[256]{0:T(256)S(1)}, f32[256]{0:T(256)S(1)}) all-reduce(f32[256]{0:T(256)S(1)} %dynamic-update-slice.2, f32[256]{0:T(256)S(1)} %dynamic-update-slice.3), channel_id=4, replica_groups=mesh['tm'=8,'row'=4,'col'=8] {'tm'}, use_global_device_ids=true, to_apply=%add.2 | all-reduce | flops 512 | bytes 4096
  199.0 2.9 %collective-permute-start.5 = (bf16[2,16,24,256]{3,2,1,0:T(8,128)(2,1)S(1)}, bf16[2,16,24,256]{3,2,1,0:T(8,128)(2,1)S(1)}, u32[]{:S(2)}, u32[]{:S(2)}) collective-permute-start(bf16[2,16,24,256]{3,2,1,0:T(8,128)(2,1)S(1)} %slice.427), channel_id=1, source_target_pairs={{0,32},{32,64},{64,96},{96,128},{128,160},{160,192},{192,224},{1,3... | collective-permute-start | bytes 1179656 | tf_op jit(solution)/shard_map/ppermute | solution.py:29
  201.8 2.3 fusion.19
  204.2 4.5 %collective-permute-done.5 = bf16[2,16,24,256]{3,2,1,0:T(8,128)(2,1)S(1)} collective-permute-done((bf16[2,16,24,256]{3,2,1,0:T(8,128)(2,1)S(1)}, bf16[2,16,24,256]{3,2,1,0:T(8,128)(2,1)S(1)}, u32[]{:S(2)}, u32[]{:S(2)}) %collective-permute-start.5) | collective-permute-done | bytes 393248 | tf_op jit(solution)/shard_map/ppermute | solution.py:29
  208.7 10.0 %collective-permute-start.7 = (bf16[6,1,24,256]{3,2,1,0:T(8,128)(2,1)S(1)}, bf16[6,1,24,256]{3,2,1,0:T(8,128)(2,1)S(1)}, u32[]{:S(2)}, u32[]{:S(2)}) collective-permute-start(bf16[6,1,24,256]{3,2,1,0:T(8,128)(2,1)S(1)} %get-tuple-element.392), channel_id=1, source_target_pairs={{8,0},{16,8},{24,16},{9,1},{17,9},{25,17},{10,2},{18,10},{26,18},{... | collective-permute-start | bytes 221192 | tf_op jit(solution)/shard_map/ppermute | solution.py:40
  218.7 1.9 collective-permute-start.6
  220.9 4.1 %collective-permute-done.6 = bf16[6,1,24,256]{3,2,1,0:T(8,128)(2,1)S(1)} collective-permute-done((bf16[6,1,24,256]{3,2,1,0:T(8,128)(2,1)S(1)}, bf16[6,1,24,256]{3,2,1,0:T(8,128)(2,1)S(1)}, u32[]{:S(2)}, u32[]{:S(2)}) %collective-permute-start.6) | collective-permute-done | bytes 73760 | tf_op jit(solution)/shard_map/ppermute | solution.py:39
  225.1 1.9 collective-permute-start.9
  227.1 2.4 collective-permute-start.8
  230.4 6.6 %collective-permute-done.8 = bf16[6,18,1,256]{3,2,1,0:T(2,128)(2,1)S(1)} collective-permute-done((bf16[6,18,1,256]{3,2,1,0:T(2,128)(2,1)S(1)}, bf16[6,18,1,256]{3,2,1,0:T(2,128)(2,1)S(1)}, u32[]{:S(2)}, u32[]{:S(2)}) %collective-permute-start.8) | collective-permute-done | bytes 55328 | tf_op jit(solution)/shard_map/ppermute | solution.py:39
  237.1 1.2 pad_maximum_fusion.19
  238.9 5.4 %fusion.21 = (bf16[4,16,24,256]{3,2,1,0:T(8,128)(2,1)S(1)}, bf16[4,16,24,256]{3,2,1,0:T(8,128)(2,1)S(1)}, bf16[4,16,24,256]{3,2,1,0:T(8,128)(2,1)S(1)}, bf16[4,1...) fusion(bf16[6,18,25,256]{3,2,1,0:T(8,128)(2,1)S(1)} %get-tuple-, ...), kind=kLoop, calls=%fused_computation.99 | loop fusion | bytes 14155776 | tf_op jit(solution)/shard_map/slice | solution.py:107
  252.9 1.2 broadcast_in_dim.27
  254.2 3.9 %broadcast_in_dim.28 = bf16[4,32,24,2,256]{4,3,2,1,0:T(2,128)(2,1)S(1)} broadcast(bf16[4,32,24,256]{3,2,1,0:T(8,128)(2,1)} %bitcast.108), dimensions={0,1,2,4} | broadcast | bytes 4718592 | tf_op jit(solution)/shard_map/broadcast_in_dim | solution.py:125
  258.0 3.2 %reshape.109 = bf16[4,32,48,256]{3,2,1,0:T(8,128)(2,1)} reshape(bf16[4,32,24,2,256]{4,3,2,1,0:T(2,128)(2,1)S(1)} %broadcast_in_dim.28) | data formatting | bytes 6291456 | tf_op jit(solution)/shard_map/reshape | solution.py:125
  (117 shorter events, 25.1 us)
Async XLA Ops:
  76.5 9.7 %collective-permute-start = (bf16[2,16,24,256]{3,2,1,0:T(8,128)(2,1)S(1)}, bf16[2,16,24,256]{3,2,1,0:T(8,128)(2,1)S(1)}, u32[]{:S(2)}, u32[]{:S(2)}) collective-permute-start(bf16[2,16,24,256]{3,2,1,0:T(8,128)(2,1)S(1)} %slice.400), channel_id=1, source_target_pairs={{0,32},{32,64},{64,96},{96,128},{128,160},{160,192},{192,224},{1,3... | collective-permute-start | bytes 1179656 | tf_op jit(solution)/shard_map/ppermute | solution.py:29
  86.2 15.6 %collective-permute-start.2 = (bf16[6,1,24,256]{3,2,1,0:T(8,128)(2,1)S(1)}, bf16[6,1,24,256]{3,2,1,0:T(8,128)(2,1)S(1)}, u32[]{:S(2)}, u32[]{:S(2)}) collective-permute-start(bf16[6,1,24,256]{3,2,1,0:T(8,128)(2,1)S(1)} %get-tuple-element.396), channel_id=1, source_target_pairs={{8,0},{16,8},{24,16},{9,1},{17,9},{25,17},{10,2},{18,10},{26,18},{... | collective-permute-start | bytes 221192 | tf_op jit(solution)/shard_map/ppermute | solution.py:40
  99.6 6.2 %collective-permute-start.1 = (bf16[6,1,24,256]{3,2,1,0:T(8,128)(2,1)S(1)}, bf16[6,1,24,256]{3,2,1,0:T(8,128)(2,1)S(1)}, u32[]{:S(2)}, u32[]{:S(2)}) collective-permute-start(bf16[6,1,24,256]{3,2,1,0:T(8,128)(2,1)S(1)} %get-tuple-element.395), channel_id=1, source_target_pairs={{0,8},{8,16},{16,24},{1,9},{9,17},{17,25},{2,10},{10,18},{18,26},{... | collective-permute-start | bytes 221192 | tf_op jit(solution)/shard_map/ppermute | solution.py:39
  106.0 5.5 %collective-permute-start.4 = (bf16[6,18,1,256]{3,2,1,0:T(2,128)(2,1)S(1)}, bf16[6,18,1,256]{3,2,1,0:T(2,128)(2,1)S(1)}, u32[]{:S(2)}, u32[]{:S(2)}) collective-permute-start(bf16[6,18,1,256]{3,2,1,0:T(2,128)(2,1)S(1)} %get-tuple-element.375), channel_id=1, source_target_pairs={{1,0},{2,1},{3,2},{4,3},{5,4},{6,5},{7,6},{9,8},{10,9},{11,10},{12... | collective-permute-start | bytes 165896 | tf_op jit(solution)/shard_map/ppermute | solution.py:40
  107.9 10.0 %collective-permute-start.3 = (bf16[6,18,1,256]{3,2,1,0:T(2,128)(2,1)S(1)}, bf16[6,18,1,256]{3,2,1,0:T(2,128)(2,1)S(1)}, u32[]{:S(2)}, u32[]{:S(2)}) collective-permute-start(bf16[6,18,1,256]{3,2,1,0:T(2,128)(2,1)S(1)} %get-tuple-element.376), channel_id=1, source_target_pairs={{0,1},{1,2},{2,3},{3,4},{4,5},{5,6},{6,7},{8,9},{9,10},{10,11},{11... | collective-permute-start | bytes 165896 | tf_op jit(solution)/shard_map/ppermute | solution.py:39
  132.3 66.2 %copy-start.3 = (f32[256]{0:T(256)S(1)}, f32[256]{0:T(256)}, u32[]{:S(2)}) copy-start(f32[256]{0:T(256)} %param.16) | copy-start | bytes 3076
  132.3 66.2 %copy-start.1 = (f32[256]{0:T(256)S(1)}, f32[256]{0:T(256)}, u32[]{:S(2)}) copy-start(f32[256]{0:T(256)} %param.17) | copy-start | bytes 3076
  199.0 9.7 %collective-permute-start.5 = (bf16[2,16,24,256]{3,2,1,0:T(8,128)(2,1)S(1)}, bf16[2,16,24,256]{3,2,1,0:T(8,128)(2,1)S(1)}, u32[]{:S(2)}, u32[]{:S(2)}) collective-permute-start(bf16[2,16,24,256]{3,2,1,0:T(8,128)(2,1)S(1)} %slice.427), channel_id=1, source_target_pairs={{0,32},{32,64},{64,96},{96,128},{128,160},{160,192},{192,224},{1,3... | collective-permute-start | bytes 1179656 | tf_op jit(solution)/shard_map/ppermute | solution.py:29
  208.7 12.2 %collective-permute-start.7 = (bf16[6,1,24,256]{3,2,1,0:T(8,128)(2,1)S(1)}, bf16[6,1,24,256]{3,2,1,0:T(8,128)(2,1)S(1)}, u32[]{:S(2)}, u32[]{:S(2)}) collective-permute-start(bf16[6,1,24,256]{3,2,1,0:T(8,128)(2,1)S(1)} %get-tuple-element.392), channel_id=1, source_target_pairs={{8,0},{16,8},{24,16},{9,1},{17,9},{25,17},{10,2},{18,10},{26,18},{... | collective-permute-start | bytes 221192 | tf_op jit(solution)/shard_map/ppermute | solution.py:40
  218.7 6.2 %collective-permute-start.6 = (bf16[6,1,24,256]{3,2,1,0:T(8,128)(2,1)S(1)}, bf16[6,1,24,256]{3,2,1,0:T(8,128)(2,1)S(1)}, u32[]{:S(2)}, u32[]{:S(2)}) collective-permute-start(bf16[6,1,24,256]{3,2,1,0:T(8,128)(2,1)S(1)} %get-tuple-element.391), channel_id=1, source_target_pairs={{0,8},{8,16},{16,24},{1,9},{9,17},{17,25},{2,10},{10,18},{18,26},{... | collective-permute-start | bytes 221192 | tf_op jit(solution)/shard_map/ppermute | solution.py:39
  225.1 5.3 %collective-permute-start.9 = (bf16[6,18,1,256]{3,2,1,0:T(2,128)(2,1)S(1)}, bf16[6,18,1,256]{3,2,1,0:T(2,128)(2,1)S(1)}, u32[]{:S(2)}, u32[]{:S(2)}) collective-permute-start(bf16[6,18,1,256]{3,2,1,0:T(2,128)(2,1)S(1)} %get-tuple-element.371), channel_id=1, source_target_pairs={{1,0},{2,1},{3,2},{4,3},{5,4},{6,5},{7,6},{9,8},{10,9},{11,10},{12... | collective-permute-start | bytes 165896 | tf_op jit(solution)/shard_map/ppermute | solution.py:40
  227.1 10.0 %collective-permute-start.8 = (bf16[6,18,1,256]{3,2,1,0:T(2,128)(2,1)S(1)}, bf16[6,18,1,256]{3,2,1,0:T(2,128)(2,1)S(1)}, u32[]{:S(2)}, u32[]{:S(2)}) collective-permute-start(bf16[6,18,1,256]{3,2,1,0:T(2,128)(2,1)S(1)} %get-tuple-element.372), channel_id=1, source_target_pairs={{0,1},{1,2},{2,3},{3,4},{4,5},{5,6},{6,7},{8,9},{9,10},{10,11},{11... | collective-permute-start | bytes 165896 | tf_op jit(solution)/shard_map/ppermute | solution.py:39
  251.6 1.1 copy-start
  251.6 1.1 copy-start.2
where the time goes:
time: 262 us; the launch traced here: 261 us
  blocking collectives  133 us (51%)
  starting transfers between devices  41.9 us (16%)
  waiting for transfers between devices  30.1 us (11%)
  local copies, waits for them, and re-layouts  29.3 us (11%)
  matrix products  14.1 us (5%)
  other arithmetic  11.4 us (4%)
    psum x2, blocking collectives, span_moments(): tile_sum, tile_square = lax.psum((local_sum, local_square), ('row', 'col'))  99.8 us
    unnamed x2, blocking collectives  33 us
    ppermute x4, starting transfers between devices, extended(): after = lax.ppermute(leading, axis, down)  27.3 us
    ppermute x4, waiting for transfers between devices, extended(): before = lax.ppermute(last, axis, up)  21.3 us
    dot_general x18, matrix products, conv_block(): jnp.dot(stacked.reshape(-1, 3 * channels), kernel[:, tap_row, tap_col].re...  14.1 us
    slice x7, local copies, waits for them, and re-layouts, conv_block(): window[tap_time:tap_time + span_frames]  12.4 us
    ppermute x2, waiting for transfers between devices, from_behind(): return lax.ppermute(block, axis, route)  8.84 us
    ppermute x4, starting transfers between devices, extended(): before = lax.ppermute(last, axis, up)  8.83 us
  transfers between devices with their start and end apart: 10, of which 6 were waited for; matrix products, arithmetic and copies ran while one was open for 3% of the time, Pallas kernels for 0%

commit v1 on v0

--- a/solution.py
+++ b/solution.py
@@ -58,7 +58,7 @@
     local_sum = jnp.sum(grouped, axis=(0, 2))
     local_square = jnp.sum(grouped * grouped, axis=(0, 2))
     span_index = lax.axis_index("tm")
-    tile_sum, tile_square = lax.psum((local_sum, local_square), ("row", "col"))
+    tile_sum, tile_square = lax.psum(lax.psum((local_sum, local_square), "col"), "row")
     empty_vec = jnp.zeros_like(tile_sum)
     prior_sum, prior_square = entering(
         (tile_sum, tile_square), "tm", add_pair, (empty_vec, empty_vec)

time: 262 us -> 180 us (0.69)
  blocking collectives: 133 us -> 71 us
  starting transfers between devices: 41.9 us -> 27.2 us
  waiting for transfers between devices: 30.1 us -> 24.5 us
    psum x2 -> x4, blocking collectives: 99.8 us -> 38 us  [the longest x2 21.9 us: span_moments(): lax.psum((local_sum, local_square), 'col')]
    ppermute x4, starting transfers between devices: 27.3 us -> 12.5 us  [extended(): after = lax.ppermute(leading, axis, down)]
    ppermute x4, waiting for transfers between devices: 21.3 us -> 15.7 us  [extended(): before = lax.ppermute(last, axis, up)]
  transfers between devices with their start and end apart: 10 -> 10, of which waited for: 6 -> 6; matrix products, arithmetic and copies ran while one was open for 3% -> 4% of each run, Pallas kernels for 0% -> 0%
where the time goes in v1:
time: 180 us; the launch traced here: 179 us
  blocking collectives  71 us (39%)
  local copies, waits for them, and re-layouts  29.2 us (16%)
  starting transfers between devices  27.2 us (15%)
  waiting for transfers between devices  24.5 us (14%)
  matrix products  14.1 us (8%)
  other arithmetic  11.4 us (6%)
    unnamed x2, blocking collectives  33 us
    psum x2, blocking collectives, span_moments(): lax.psum((local_sum, local_square), 'col')  21.9 us
    psum x2, blocking collectives, span_moments(): lax.psum(lax.psum((local_sum, local_square), 'col'), 'row')  16.1 us
    ppermute x4, waiting for transfers between devices, extended(): before = lax.ppermute(last, axis, up)  15.7 us
    dot_general x18, matrix products, conv_block(): jnp.dot(stacked.reshape(-1, 3 * channels), kernel[:, tap_row, tap_col].re...  14.1 us
    ppermute x4, starting transfers between devices, extended(): after = lax.ppermute(leading, axis, down)  12.5 us
    slice x7, local copies, waits for them, and re-layouts, conv_block(): window[tap_time:tap_time + span_frames]  12.4 us
    ppermute x2, waiting for transfers between devices, from_behind(): return lax.ppermute(block, axis, route)  8.84 us
  transfers between devices with their start and end apart: 10, of which 6 were waited for; matrix products, arithmetic and copies ran while one was open for 4% of the time, Pallas kernels for 0%

profile of v1, /device:TPU:42, one launch (start us, length us, event | category | flops | bytes accessed | tf_op | source)
XLA Modules:
  0.0 179.0 jit_solution(15690506912449059427)
XLA Ops:
  0.0 1.4 fusion.6
  1.8 11.7 %all-reduce.5 = (f32[32]{0:T(128)S(1)}, f32[32]{0:T(128)S(1)}) all-reduce(f32[32]{0:T(128)S(1)} %reduce_sum.51, f32[32]{0:T(128)S(1)} %reduce_sum.54), channel_id=1, replica_groups=mesh['tm'=8,'row'=4,'col'=8] {'col'}, use_global_device_ids=true, to_apply=%region_2.0 | all-reduce | flops 64 | bytes 512 | tf_op jit(solution)/shard_map/psum | solution.py:61
  13.5 8.7 %all-reduce.9 = (f32[32]{0:T(128)S(1)}, f32[32]{0:T(128)S(1)}) all-reduce(f32[32]{0:T(128)S(1)} %get-tuple-element.301, f32[32]{0:T(128)S(1)} %get-tuple-element.302), channel_id=1, replica_groups=mesh['tm'=8,'row'=4,'col'=8] {'row'}, use_global_device_ids=true, to_apply=%region_3.0 | all-reduce | flops 64 | bytes 512 | tf_op jit(solution)/shard_map/psum | solution.py:61
  22.1 1.3 dynamic-slice
  24.4 17.9 %all-reduce.7 = (f32[256]{0:T(256)S(1)}, f32[256]{0:T(256)S(1)}) all-reduce(f32[256]{0:T(256)S(1)} %dynamic-update-slice, f32[256]{0:T(256)S(1)} %dynamic-update-slice.1), channel_id=2, replica_groups=mesh['tm'=8,'row'=4,'col'=8] {'tm'}, use_global_device_ids=true, to_apply=%add | all-reduce | flops 512 | bytes 4096
  43.8 1.6 fusion.14
  45.5 2.9 %collective-permute-start = (bf16[2,16,24,256]{3,2,1,0:T(8,128)(2,1)S(1)}, bf16[2,16,24,256]{3,2,1,0:T(8,128)(2,1)S(1)}, u32[]{:S(2)}, u32[]{:S(2)}) collective-permute-start(bf16[2,16,24,256]{3,2,1,0:T(8,128)(2,1)S(1)} %slice.400), channel_id=1, source_target_pairs={{0,32},{32,64},{64,96},{96,128},{128,160},{160,192},{192,224},{1,3... | collective-permute-start | bytes 1179656 | tf_op jit(solution)/shard_map/ppermute | solution.py:29
  48.4 2.3 %fusion.20 = (bf16[3,1,1,256,256]{4,3,2,1,0:T(8,128)(2,1)S(1)}, bf16[3,1,1,256,256]{4,3,2,1,0:T(8,128)(2,1)S(1)}, bf16[3,1,1,256,256]{4,3,2,1,0:T(8,128)(2,1)S(1...) fusion(bf16[3,3,3,256,256]{4,3,2,1,0:T(8,128)(2,1)} %param.15), kind=kLoop, calls=%fused_computation.98 | loop fusion | bytes 7077888 | tf_op jit(solution)/shard_map/slice | solution.py:111
  50.8 4.4 %collective-permute-done = bf16[2,16,24,256]{3,2,1,0:T(8,128)(2,1)S(1)} collective-permute-done((bf16[2,16,24,256]{3,2,1,0:T(8,128)(2,1)S(1)}, bf16[2,16,24,256]{3,2,1,0:T(8,128)(2,1)S(1)}, u32[]{:S(2)}, u32[]{:S(2)}) %collective-permute-start) | collective-permute-done | bytes 393248 | tf_op jit(solution)/shard_map/ppermute | solution.py:29
  55.2 4.4 %collective-permute-start.2 = (bf16[6,1,24,256]{3,2,1,0:T(8,128)(2,1)S(1)}, bf16[6,1,24,256]{3,2,1,0:T(8,128)(2,1)S(1)}, u32[]{:S(2)}, u32[]{:S(2)}) collective-permute-start(bf16[6,1,24,256]{3,2,1,0:T(8,128)(2,1)S(1)} %get-tuple-element.400), channel_id=1, source_target_pairs={{8,0},{16,8},{24,16},{9,1},{17,9},{25,17},{10,2},{18,10},{26,18},{... | collective-permute-start | bytes 221192 | tf_op jit(solution)/shard_map/ppermute | solution.py:40
  59.6 1.9 %collective-permute-start.1 = (bf16[6,1,24,256]{3,2,1,0:T(8,128)(2,1)S(1)}, bf16[6,1,24,256]{3,2,1,0:T(8,128)(2,1)S(1)}, u32[]{:S(2)}, u32[]{:S(2)}) collective-permute-start(bf16[6,1,24,256]{3,2,1,0:T(8,128)(2,1)S(1)} %get-tuple-element.399), channel_id=1, source_target_pairs={{0,8},{8,16},{16,24},{1,9},{9,17},{17,25},{2,10},{10,18},{18,26},{... | collective-permute-start | bytes 221192 | tf_op jit(solution)/shard_map/ppermute | solution.py:39
  61.7 4.1 %collective-permute-done.1 = bf16[6,1,24,256]{3,2,1,0:T(8,128)(2,1)S(1)} collective-permute-done((bf16[6,1,24,256]{3,2,1,0:T(8,128)(2,1)S(1)}, bf16[6,1,24,256]{3,2,1,0:T(8,128)(2,1)S(1)}, u32[]{:S(2)}, u32[]{:S(2)}) %collective-permute-start.1) | collective-permute-done | bytes 73760 | tf_op jit(solution)/shard_map/ppermute | solution.py:39
  66.0 1.9 %collective-permute-start.4 = (bf16[6,18,1,256]{3,2,1,0:T(2,128)(2,1)S(1)}, bf16[6,18,1,256]{3,2,1,0:T(2,128)(2,1)S(1)}, u32[]{:S(2)}, u32[]{:S(2)}) collective-permute-start(bf16[6,18,1,256]{3,2,1,0:T(2,128)(2,1)S(1)} %get-tuple-element.379), channel_id=1, source_target_pairs={{1,0},{2,1},{3,2},{4,3},{5,4},{6,5},{7,6},{9,8},{10,9},{11,10},{12... | collective-permute-start | bytes 165896 | tf_op jit(solution)/shard_map/ppermute | solution.py:40
  67.9 2.6 %collective-permute-start.3 = (bf16[6,18,1,256]{3,2,1,0:T(2,128)(2,1)S(1)}, bf16[6,18,1,256]{3,2,1,0:T(2,128)(2,1)S(1)}, u32[]{:S(2)}, u32[]{:S(2)}) collective-permute-start(bf16[6,18,1,256]{3,2,1,0:T(2,128)(2,1)S(1)} %get-tuple-element.380), channel_id=1, source_target_pairs={{0,1},{1,2},{2,3},{3,4},{4,5},{5,6},{6,7},{8,9},{9,10},{10,11},{11... | collective-permute-start | bytes 165896 | tf_op jit(solution)/shard_map/ppermute | solution.py:39
  71.5 4.4 %collective-permute-done.3 = bf16[6,18,1,256]{3,2,1,0:T(2,128)(2,1)S(1)} collective-permute-done((bf16[6,18,1,256]{3,2,1,0:T(2,128)(2,1)S(1)}, bf16[6,18,1,256]{3,2,1,0:T(2,128)(2,1)S(1)}, u32[]{:S(2)}, u32[]{:S(2)}) %collective-permute-start.3) | collective-permute-done | bytes 55328 | tf_op jit(solution)/shard_map/ppermute | solution.py:39
  75.8 1.2 pad_maximum_fusion.18
  77.6 5.1 %fusion.23 = (bf16[4,16,24,256]{3,2,1,0:T(8,128)(2,1)S(1)}, bf16[4,16,24,256]{3,2,1,0:T(8,128)(2,1)S(1)}, bf16[4,16,24,256]{3,2,1,0:T(8,128)(2,1)S(1)}, bf16[4,1...) fusion(bf16[6,18,25,256]{3,2,1,0:T(8,128)(2,1)S(1)} %get-tuple-, ...), kind=kLoop, calls=%fused_computation.101 | loop fusion | bytes 14155776 | tf_op jit(solution)/shard_map/slice | solution.py:107
  91.4 10.3 %all-reduce.4 = (f32[32]{0:T(128)S(1)}, f32[32]{0:T(128)S(1)}) all-reduce(f32[32]{0:T(128)S(1)} %reduce_sum.72, f32[32]{0:T(128)S(1)} %reduce_sum.75), channel_id=1, replica_groups=mesh['tm'=8,'row'=4,'col'=8] {'col'}, use_global_device_ids=true, to_apply=%region_12.13 | all-reduce | flops 64 | bytes 512 | tf_op jit(solution)/shard_map/psum | solution.py:61
  101.7 7.4 %all-reduce.8 = (f32[32]{0:T(128)S(1)}, f32[32]{0:T(128)S(1)}) all-reduce(f32[32]{0:T(128)S(1)} %get-tuple-element.299, f32[32]{0:T(128)S(1)} %get-tuple-element.300), channel_id=1, replica_groups=mesh['tm'=8,'row'=4,'col'=8] {'row'}, use_global_device_ids=true, to_apply=%region_13.14 | all-reduce | flops 64 | bytes 512 | tf_op jit(solution)/shard_map/psum | solution.py:61
  109.5 15.1 %all-reduce.6 = (f32[256]{0:T(256)S(1)}, f32[256]{0:T(256)S(1)}) all-reduce(f32[256]{0:T(256)S(1)} %dynamic-update-slice.2, f32[256]{0:T(256)S(1)} %dynamic-update-slice.3), channel_id=4, replica_groups=mesh['tm'=8,'row'=4,'col'=8] {'tm'}, use_global_device_ids=true, to_apply=%add.2 | all-reduce | flops 512 | bytes 4096
  125.9 2.9 %collective-permute-start.5 = (bf16[2,16,24,256]{3,2,1,0:T(8,128)(2,1)S(1)}, bf16[2,16,24,256]{3,2,1,0:T(8,128)(2,1)S(1)}, u32[]{:S(2)}, u32[]{:S(2)}) collective-permute-start(bf16[2,16,24,256]{3,2,1,0:T(8,128)(2,1)S(1)} %slice.427), channel_id=1, source_target_pairs={{0,32},{32,64},{64,96},{96,128},{128,160},{160,192},{192,224},{1,3... | collective-permute-start | bytes 1179656 | tf_op jit(solution)/shard_map/ppermute | solution.py:29
  128.8 2.3 %fusion.19 = (bf16[3,1,1,256,256]{4,3,2,1,0:T(8,128)(2,1)S(1)}, bf16[3,1,1,256,256]{4,3,2,1,0:T(8,128)(2,1)S(1)}, bf16[3,1,1,256,256]{4,3,2,1,0:T(8,128)(2,1)S(1...) fusion(bf16[3,3,3,256,256]{4,3,2,1,0:T(8,128)(2,1)} %param.18), kind=kLoop, calls=%fused_computation.97 | loop fusion | bytes 7077888 | tf_op jit(solution)/shard_map/slice | solution.py:111
  131.2 4.5 %collective-permute-done.5 = bf16[2,16,24,256]{3,2,1,0:T(8,128)(2,1)S(1)} collective-permute-done((bf16[2,16,24,256]{3,2,1,0:T(8,128)(2,1)S(1)}, bf16[2,16,24,256]{3,2,1,0:T(8,128)(2,1)S(1)}, u32[]{:S(2)}, u32[]{:S(2)}) %collective-permute-start.5) | collective-permute-done | bytes 393248 | tf_op jit(solution)/shard_map/ppermute | solution.py:29
  135.6 4.3 %collective-permute-start.7 = (bf16[6,1,24,256]{3,2,1,0:T(8,128)(2,1)S(1)}, bf16[6,1,24,256]{3,2,1,0:T(8,128)(2,1)S(1)}, u32[]{:S(2)}, u32[]{:S(2)}) collective-permute-start(bf16[6,1,24,256]{3,2,1,0:T(8,128)(2,1)S(1)} %get-tuple-element.396), channel_id=1, source_target_pairs={{8,0},{16,8},{24,16},{9,1},{17,9},{25,17},{10,2},{18,10},{26,18},{... | collective-permute-start | bytes 221192 | tf_op jit(solution)/shard_map/ppermute | solution.py:40
  139.9 1.9 %collective-permute-start.6 = (bf16[6,1,24,256]{3,2,1,0:T(8,128)(2,1)S(1)}, bf16[6,1,24,256]{3,2,1,0:T(8,128)(2,1)S(1)}, u32[]{:S(2)}, u32[]{:S(2)}) collective-permute-start(bf16[6,1,24,256]{3,2,1,0:T(8,128)(2,1)S(1)} %get-tuple-element.395), channel_id=1, source_target_pairs={{0,8},{8,16},{16,24},{1,9},{9,17},{17,25},{2,10},{10,18},{18,26},{... | collective-permute-start | bytes 221192 | tf_op jit(solution)/shard_map/ppermute | solution.py:39
  142.1 4.1 %collective-permute-done.6 = bf16[6,1,24,256]{3,2,1,0:T(8,128)(2,1)S(1)} collective-permute-done((bf16[6,1,24,256]{3,2,1,0:T(8,128)(2,1)S(1)}, bf16[6,1,24,256]{3,2,1,0:T(8,128)(2,1)S(1)}, u32[]{:S(2)}, u32[]{:S(2)}) %collective-permute-start.6) | collective-permute-done | bytes 73760 | tf_op jit(solution)/shard_map/ppermute | solution.py:39
  146.4 1.9 %collective-permute-start.9 = (bf16[6,18,1,256]{3,2,1,0:T(2,128)(2,1)S(1)}, bf16[6,18,1,256]{3,2,1,0:T(2,128)(2,1)S(1)}, u32[]{:S(2)}, u32[]{:S(2)}) collective-permute-start(bf16[6,18,1,256]{3,2,1,0:T(2,128)(2,1)S(1)} %get-tuple-element.375), channel_id=1, source_target_pairs={{1,0},{2,1},{3,2},{4,3},{5,4},{6,5},{7,6},{9,8},{10,9},{11,10},{12... | collective-permute-start | bytes 165896 | tf_op jit(solution)/shard_map/ppermute | solution.py:40
  148.3 2.4 %collective-permute-start.8 = (bf16[6,18,1,256]{3,2,1,0:T(2,128)(2,1)S(1)}, bf16[6,18,1,256]{3,2,1,0:T(2,128)(2,1)S(1)}, u32[]{:S(2)}, u32[]{:S(2)}) collective-permute-start(bf16[6,18,1,256]{3,2,1,0:T(2,128)(2,1)S(1)} %get-tuple-element.376), channel_id=1, source_target_pairs={{0,1},{1,2},{2,3},{3,4},{4,5},{5,6},{6,7},{8,9},{9,10},{10,11},{11... | collective-permute-start | bytes 165896 | tf_op jit(solution)/shard_map/ppermute | solution.py:39
  151.7 3.2 %collective-permute-done.8 = bf16[6,18,1,256]{3,2,1,0:T(2,128)(2,1)S(1)} collective-permute-done((bf16[6,18,1,256]{3,2,1,0:T(2,128)(2,1)S(1)}, bf16[6,18,1,256]{3,2,1,0:T(2,128)(2,1)S(1)}, u32[]{:S(2)}, u32[]{:S(2)}) %collective-permute-start.8) | collective-permute-done | bytes 55328 | tf_op jit(solution)/shard_map/ppermute | solution.py:39
  156.6 5.4 %fusion.21 = (bf16[4,16,24,256]{3,2,1,0:T(8,128)(2,1)S(1)}, bf16[4,16,24,256]{3,2,1,0:T(8,128)(2,1)S(1)}, bf16[4,16,24,256]{3,2,1,0:T(8,128)(2,1)S(1)}, bf16[4,1...) fusion(bf16[6,18,25,256]{3,2,1,0:T(8,128)(2,1)S(1)} %get-tuple-, ...), kind=kLoop, calls=%fused_computation.99 | loop fusion | bytes 14155776 | tf_op jit(solution)/shard_map/slice | solution.py:107
  171.9 3.9 %broadcast_in_dim.28 = bf16[4,32,24,2,256]{4,3,2,1,0:T(2,128)(2,1)S(1)} broadcast(bf16[4,32,24,256]{3,2,1,0:T(8,128)(2,1)} %bitcast.108), dimensions={0,1,2,4} | broadcast | bytes 4718592 | tf_op jit(solution)/shard_map/broadcast_in_dim | solution.py:125
  175.8 3.2 %reshape.109 = bf16[4,32,48,256]{3,2,1,0:T(8,128)(2,1)} reshape(bf16[4,32,24,2,256]{4,3,2,1,0:T(2,128)(2,1)S(1)} %broadcast_in_dim.28) | data formatting | bytes 6291456 | tf_op jit(solution)/shard_map/reshape | solution.py:125
  (119 shorter events, 27.6 us)
Async XLA Ops:
  45.5 9.7 %collective-permute-start = (bf16[2,16,24,256]{3,2,1,0:T(8,128)(2,1)S(1)}, bf16[2,16,24,256]{3,2,1,0:T(8,128)(2,1)S(1)}, u32[]{:S(2)}, u32[]{:S(2)}) collective-permute-start(bf16[2,16,24,256]{3,2,1,0:T(8,128)(2,1)S(1)} %slice.400), channel_id=1, source_target_pairs={{0,32},{32,64},{64,96},{96,128},{128,160},{160,192},{192,224},{1,3... | collective-permute-start | bytes 1179656 | tf_op jit(solution)/shard_map/ppermute | solution.py:29
  55.2 6.6 %collective-permute-start.2 = (bf16[6,1,24,256]{3,2,1,0:T(8,128)(2,1)S(1)}, bf16[6,1,24,256]{3,2,1,0:T(8,128)(2,1)S(1)}, u32[]{:S(2)}, u32[]{:S(2)}) collective-permute-start(bf16[6,1,24,256]{3,2,1,0:T(8,128)(2,1)S(1)} %get-tuple-element.400), channel_id=1, source_target_pairs={{8,0},{16,8},{24,16},{9,1},{17,9},{25,17},{10,2},{18,10},{26,18},{... | collective-permute-start | bytes 221192 | tf_op jit(solution)/shard_map/ppermute | solution.py:40
  59.6 6.2 %collective-permute-start.1 = (bf16[6,1,24,256]{3,2,1,0:T(8,128)(2,1)S(1)}, bf16[6,1,24,256]{3,2,1,0:T(8,128)(2,1)S(1)}, u32[]{:S(2)}, u32[]{:S(2)}) collective-permute-start(bf16[6,1,24,256]{3,2,1,0:T(8,128)(2,1)S(1)} %get-tuple-element.399), channel_id=1, source_target_pairs={{0,8},{8,16},{16,24},{1,9},{9,17},{17,25},{2,10},{10,18},{18,26},{... | collective-permute-start | bytes 221192 | tf_op jit(solution)/shard_map/ppermute | solution.py:39
  66.0 5.5 %collective-permute-start.4 = (bf16[6,18,1,256]{3,2,1,0:T(2,128)(2,1)S(1)}, bf16[6,18,1,256]{3,2,1,0:T(2,128)(2,1)S(1)}, u32[]{:S(2)}, u32[]{:S(2)}) collective-permute-start(bf16[6,18,1,256]{3,2,1,0:T(2,128)(2,1)S(1)} %get-tuple-element.379), channel_id=1, source_target_pairs={{1,0},{2,1},{3,2},{4,3},{5,4},{6,5},{7,6},{9,8},{10,9},{11,10},{12... | collective-permute-start | bytes 165896 | tf_op jit(solution)/shard_map/ppermute | solution.py:40
  67.9 7.9 %collective-permute-start.3 = (bf16[6,18,1,256]{3,2,1,0:T(2,128)(2,1)S(1)}, bf16[6,18,1,256]{3,2,1,0:T(2,128)(2,1)S(1)}, u32[]{:S(2)}, u32[]{:S(2)}) collective-permute-start(bf16[6,18,1,256]{3,2,1,0:T(2,128)(2,1)S(1)} %get-tuple-element.380), channel_id=1, source_target_pairs={{0,1},{1,2},{2,3},{3,4},{4,5},{5,6},{6,7},{8,9},{9,10},{10,11},{11... | collective-permute-start | bytes 165896 | tf_op jit(solution)/shard_map/ppermute | solution.py:39
  90.2 35.3 %copy-start.3 = (f32[256]{0:T(256)S(1)}, f32[256]{0:T(256)}, u32[]{:S(2)}) copy-start(f32[256]{0:T(256)} %param.16) | copy-start | bytes 3076
  90.2 35.3 %copy-start.1 = (f32[256]{0:T(256)S(1)}, f32[256]{0:T(256)}, u32[]{:S(2)}) copy-start(f32[256]{0:T(256)} %param.17) | copy-start | bytes 3076
  125.9 9.7 %collective-permute-start.5 = (bf16[2,16,24,256]{3,2,1,0:T(8,128)(2,1)S(1)}, bf16[2,16,24,256]{3,2,1,0:T(8,128)(2,1)S(1)}, u32[]{:S(2)}, u32[]{:S(2)}) collective-permute-start(bf16[2,16,24,256]{3,2,1,0:T(8,128)(2,1)S(1)} %slice.427), channel_id=1, source_target_pairs={{0,32},{32,64},{64,96},{96,128},{128,160},{160,192},{192,224},{1,3... | collective-permute-start | bytes 1179656 | tf_op jit(solution)/shard_map/ppermute | solution.py:29
  135.6 6.5 %collective-permute-start.7 = (bf16[6,1,24,256]{3,2,1,0:T(8,128)(2,1)S(1)}, bf16[6,1,24,256]{3,2,1,0:T(8,128)(2,1)S(1)}, u32[]{:S(2)}, u32[]{:S(2)}) collective-permute-start(bf16[6,1,24,256]{3,2,1,0:T(8,128)(2,1)S(1)} %get-tuple-element.396), channel_id=1, source_target_pairs={{8,0},{16,8},{24,16},{9,1},{17,9},{25,17},{10,2},{18,10},{26,18},{... | collective-permute-start | bytes 221192 | tf_op jit(solution)/shard_map/ppermute | solution.py:40
  139.9 6.2 %collective-permute-start.6 = (bf16[6,1,24,256]{3,2,1,0:T(8,128)(2,1)S(1)}, bf16[6,1,24,256]{3,2,1,0:T(8,128)(2,1)S(1)}, u32[]{:S(2)}, u32[]{:S(2)}) collective-permute-start(bf16[6,1,24,256]{3,2,1,0:T(8,128)(2,1)S(1)} %get-tuple-element.395), channel_id=1, source_target_pairs={{0,8},{8,16},{16,24},{1,9},{9,17},{17,25},{2,10},{10,18},{18,26},{... | collective-permute-start | bytes 221192 | tf_op jit(solution)/shard_map/ppermute | solution.py:39
  146.4 5.3 %collective-permute-start.9 = (bf16[6,18,1,256]{3,2,1,0:T(2,128)(2,1)S(1)}, bf16[6,18,1,256]{3,2,1,0:T(2,128)(2,1)S(1)}, u32[]{:S(2)}, u32[]{:S(2)}) collective-permute-start(bf16[6,18,1,256]{3,2,1,0:T(2,128)(2,1)S(1)} %get-tuple-element.375), channel_id=1, source_target_pairs={{1,0},{2,1},{3,2},{4,3},{5,4},{6,5},{7,6},{9,8},{10,9},{11,10},{12... | collective-permute-start | bytes 165896 | tf_op jit(solution)/shard_map/ppermute | solution.py:40
  148.3 6.5 %collective-permute-start.8 = (bf16[6,18,1,256]{3,2,1,0:T(2,128)(2,1)S(1)}, bf16[6,18,1,256]{3,2,1,0:T(2,128)(2,1)S(1)}, u32[]{:S(2)}, u32[]{:S(2)}) collective-permute-start(bf16[6,18,1,256]{3,2,1,0:T(2,128)(2,1)S(1)} %get-tuple-element.376), channel_id=1, source_target_pairs={{0,1},{1,2},{2,3},{3,4},{4,5},{5,6},{6,7},{8,9},{9,10},{10,11},{11... | collective-permute-start | bytes 165896 | tf_op jit(solution)/shard_map/ppermute | solution.py:39
  169.3 1.1 copy-start
  169.3 1.1 copy-start.2
